TPU v7x, 128 devices: a whole 4x4x4 slice. The times are simulated.
128 devices in a mesh: tm: 32 (over y, z, core), series: 4 (over x).
Axes of the slice: x: 4, y: 4, z: 4, core: 2. Of those that a mesh axis runs over, the one named last changes fastest.
Arguments:
- signal: float32 [64, 1048576], P('series', 'tm')
- valid_start: int32 [64], replicated, may hold values from 0 to 262143
- valid_end: int32 [64], replicated, may hold values from 786433 to 1048576
Outputs:
- smooth: float32 [64, 1048576], P('series', 'tm')
- slope: float32 [64, 1048576], P('series', 'tm')
- covariance: float32 [64, 64], P('series')
Inputs may be any that keep to these rules, and one draw needn't show every extreme that they name: `valid_end`: end of the valid samples of each series.
All inputs are finite; a program needn't handle non-finite values.
Results may differ from a plain program's by a relative error of at most 0.00015.
Values sent between devices are 32-bit elements; how exact they have to be, the bound alone decides.
No kernel may reach another device: no remote copies, remote signals or barrier semaphores. Data moves between devices by JAX's collectives and lax.ppermute only.
A program may use at most 64 MiB of HBM per device.

v0:
```python
import jax
import jax.numpy as jnp
from jax import lax
from jax.sharding import PartitionSpec as P

HALF = 16


def padded(cells, sides, width):
    for axis, dim in sides:
        count = lax.axis_size(axis)
        ends = count - 1
        head = lax.slice_in_dim(cells, 0, width, axis=dim)
        tail = lax.slice_in_dim(cells, cells.shape[dim] - width, cells.shape[dim], axis=dim)
        cells = jnp.concatenate(
            [
                lax.ppermute(tail, axis, [(i, (i + 1) % count) for i in range(ends)]),
                cells,
                lax.ppermute(head, axis, [((i + 1) % count, i) for i in range(ends)]),
            ],
            axis=dim,
        )
    return cells


def split_up(shard, dim, count):
    before, after = (shard.shape[:dim], shard.shape[dim + 1 :])
    return jnp.moveaxis(shard.reshape(*before, count, -1, *after), dim, 0)


def summed_on_arrival(shard, axis, dim):
    count = lax.axis_size(axis)
    tiles = lax.all_to_all(split_up(shard, dim, count), axis, 0, 0, tiled=True)
    return jnp.sum(tiles, axis=0)


def from_everyone(shard, axis):
    copies = jnp.broadcast_to(shard, (lax.axis_size(axis), *shard.shape))
    return lax.all_to_all(copies, axis, split_axis=0, concat_axis=0, tiled=True)


def over_copies(shard, axis):
    return from_everyone(shard, axis).sum(axis=0)


def cross_rows(left, right):
    return lax.dot_general(
        left,
        right,
        (((1,), (1,)), ((), ())),
        precision=lax.Precision.HIGHEST,
        preferred_element_type=jnp.float32,
    )


def held_value(field, spot):
    return jnp.take_along_axis(field, spot, axis=1)


def shards(signal, valid_start, valid_end):
    rows, width = signal.shape
    taps = 2 * HALF + 1
    offsets = jnp.arange(-HALF, HALF + 1).astype(jnp.float32)
    second = jnp.sum(offsets * offsets)
    centre_sq = second / taps
    curved = offsets * offsets - centre_sq
    fourth = jnp.sum(curved * curved)
    extended = padded(signal, (("tm", 1),), 2 * HALF)
    span = width + 2 * HALF
    level = jnp.zeros((rows, span), jnp.float32)
    tilt = jnp.zeros((rows, span), jnp.float32)
    bend = jnp.zeros((rows, span), jnp.float32)
    for m in range(taps):
        window = extended[:, m : m + span]
        level = level + window * (1.0 / taps)
        tilt = tilt + window * (offsets[m] / second)
        bend = bend + window * (curved[m] / fourth)
    begin = lax.axis_index("tm") * width
    group = lax.axis_index("series") * rows
    first = lax.dynamic_slice_in_dim(valid_start, group, rows)[:, None]
    last = lax.dynamic_slice_in_dim(valid_end, group, rows)[:, None]
    moment = begin + jnp.arange(width, dtype=jnp.int32)[None, :]
    low_centre = first + HALF
    high_centre = last - HALF - 1
    centre = jnp.clip(moment, low_centre, high_centre)
    low_spot = jnp.clip(low_centre - begin + HALF, 0, span - 1)
    high_spot = jnp.clip(high_centre - begin + HALF, 0, span - 1)
    below = moment < low_centre
    above = moment > high_centre
    along = (moment - centre).astype(jnp.float32)
    lv = jnp.where(
        below,
        held_value(level, low_spot),
        jnp.where(above, held_value(level, high_spot), level[:, HALF : HALF + width]),
    )
    tl = jnp.where(
        below,
        held_value(tilt, low_spot),
        jnp.where(above, held_value(tilt, high_spot), tilt[:, HALF : HALF + width]),
    )
    bd = jnp.where(
        below,
        held_value(bend, low_spot),
        jnp.where(above, held_value(bend, high_spot), bend[:, HALF : HALF + width]),
    )
    inside = (moment >= first) & (moment < last)
    smooth = jnp.where(inside, lv + tl * along + bd * (along * along - centre_sq), 0.0)
    slope = jnp.where(inside, HALF * (tl + 2.0 * along * bd), 0.0)
    resid = jnp.where(inside, signal - smooth, 0.0)
    mixed = lax.all_to_all(resid, "series", split_axis=1, concat_axis=0, tiled=True)
    gram = summed_on_arrival(cross_rows(mixed, mixed), "series", 0)
    gram = over_copies(gram, "tm")
    correlation = (
        jnp.minimum(last, valid_end[None, :]) - jnp.maximum(first, valid_start[None, :])
    ).astype(jnp.float32)
    return (smooth, slope, gram / correlation)


def solution(mesh):
    in_specs = (P("series", "tm"), P(), P())
    out_specs = (P("series", "tm"), P("series", "tm"), P("series", None))
    return jax.shard_map(shards, mesh=mesh, in_specs=in_specs, out_specs=out_specs, check_vma=False)
```

profile of v0, /device:TPU:1, one launch (start us, length us, event | category | flops | bytes accessed | tf_op | source)
XLA Modules:
  0.0 243.7 jit_solution(17497777037096725441)
XLA Ops:
  0.6 0.8 fusion.16
  1.4 4.9 %collective-permute-start = (f32[16,32]{1,0:T(8,128)S(1)}, f32[16,32]{1,0:T(8,128)S(1)}, u32[]{:S(2)}, u32[]{:S(2)}) collective-permute-start(f32[16,32]{1,0:T(8,128)S(1)} %get-tuple-element.11), channel_id=1, source_target_pairs={{0,4},{4,8},{8,12},{12,16},{16,20},{20,24},{24,28},{28,32},{32,36}... | collective-permute-start | bytes 6152 | tf_op jit(solution)/shard_map/ppermute | solution.py:17
  6.3 1.9 collective-permute-start.1
  8.9 0.7 fusion.17
  9.6 0.7 fusion.18
  10.3 3.1 %constant_dynamic-update-slice_fusion.1 = f32[16,32800]{1,0:T(8,128)} fusion(f32[16,32768]{1,0:T(8,128)} %param.5), kind=kLoop, calls=%fused_computation.29 | loop fusion | bytes 4194304
  14.7 0.7 fusion.19
  15.4 0.7 fusion.20
  101.8 6.4 %dynamic-update-slice.3 = f32[16,32832]{1,0:T(8,128)S(1)} dynamic-update-slice(f32[16,32832]{1,0:T(8,128)S(1)} %dynamic-update-slice.2, f32[16,32768]{1,0:T(8,128)} %param.5, s32[]{} %constant.163, s32[]{} %constant.165) | dynamic-update-slice | bytes 4194308
  108.9 19.9 %multiply_add_fusion.1 = f32[16,32800]{1,0:T(8,128)} fusion(f32[16,32800]{1,0:T(8,128)} %constant_dynamic-update-slice_fusion, f32[16,32832]{1,0:T(8,128)S(1)} %dynamic-update-slice.4, f32[16,32768]{1,0:T(8,128)} %param.5, f32[16,32]{1,0:T(8,128)S(1)} %collective-permute-done, f32[]{:T(128)S(6)} %div.236, f32[]{:T(128)S(6)} %div.235, f32[]{:T(128)S(6)} %div.234, ...), kind=kLoop, calls=%fused_computation.15 | loop fusion | flops 34636800 | bytes 71372928 | tf_op jit(solution)/shard_map/add | solution.py:76
  128.8 1.6 gather_fusion.2
  130.4 1.6 gather_fusion.3
  132.0 19.9 %multiply_add_fusion = f32[16,32800]{1,0:T(8,128)} fusion(f32[16,32800]{1,0:T(8,128)} %constant_dynamic-update-slice_fusion, f32[16,32832]{1,0:T(8,128)S(1)} %dynamic-update-slice.4, f32[16,32768]{1,0:T(8,128)} %param.5, f32[16,32]{1,0:T(8,128)S(1)} %collective-permute-done, f32[]{:T(128)S(6)} %div.270, f32[]{:T(128)S(6)} %div.269, f32[]{:T(128)S(6)} %div.268, ...), kind=kLoop, calls=%fused_computation.14 | loop fusion | flops 34636800 | bytes 71372928 | tf_op jit(solution)/shard_map/add | solution.py:77
  151.9 1.6 gather_fusion.4
  153.5 1.6 gather_fusion.5
  155.1 19.9 %add_multiply_fusion = f32[16,32800]{1,0:T(8,128)} fusion(f32[16,32800]{1,0:T(8,128)} %constant_dynamic-update-slice_fusion, f32[16,32832]{1,0:T(8,128)S(1)} %dynamic-update-slice.4, f32[16,32768]{1,0:T(8,128)} %param.5, f32[16,32]{1,0:T(8,128)S(1)} %collective-permute-done), kind=kLoop, calls=%fused_computation.13 | loop fusion | flops 17843200 | bytes 71372800 | tf_op jit(solution)/shard_map/add | solution.py:75
  175.0 1.6 gather_fusion
  176.6 1.7 gather_fusion.1
  178.2 6.0 %subtract_select_fusion = (f32[16,32768]{1,0:T(8,128)S(1)}, f32[16,32768]{1,0:T(8,128)}, f32[16,32768]{1,0:T(8,128)}) fusion(f32[16,32768]{1,0:T(8,128)} %param.5, s32[32768]{0:T(1024)S(1)} %iota_add_fusion, s32[16]{0:T(128)S(1)} %get-tuple-element.9, s32[16]{0:T(128)S(1)} %get-tuple-element.7, f32[]{:T(128)S(6)} %div.237, f32[16,32800]{1,0:T(8,128)} %multiply_add_fusion, ...), kind=kLoop, calls=%fused_computation.22 | loop fusion | flops 15204352 | bytes 14811780 | tf_op jit(solution)/shard_map/jit(_where)/select_n | solution.py:109
  184.3 29.0 %all_to_all.29 = f32[16,4,8192]{2,0,1:T(8,128)S(1)} all-to-all(f32[16,4,8192]{2,0,1:T(8,128)S(1)} %bitcast.164), channel_id=1, replica_groups=mesh['tm'=32,'series'=4] {'series'}, dimensions={1} | all-to-all | bytes 4194304 | tf_op jit(solution)/shard_map/all_to_all | solution.py:110
  213.4 1.8 fusion.3
  215.3 6.6 %all_to_all.30 = f32[4,1,1024]{2,1,0:T(1,128)S(1)} all-to-all(f32[4,1,1024]{2,1,0:T(1,128)S(1)} %reshape.138), channel_id=1, replica_groups=mesh['tm'=32,'series'=4] {'series'}, dimensions={0} | all-to-all | bytes 32768 | tf_op jit(solution)/shard_map/all_to_all | solution.py:33
  223.4 18.5 %all_to_all.31 = f32[32,1,1024]{2,1,0:T(1,128)S(1)} all-to-all(f32[32,1,1024]{2,1,0:T(1,128)S(1)} %reshape.140), channel_id=1, replica_groups=mesh['tm'=32,'series'=4] {'tm'}, dimensions={0} | all-to-all | bytes 262144 | tf_op jit(solution)/shard_map/all_to_all | solution.py:39
  241.9 1.0 reduce.1
  (35 shorter events, 5.1 us)
Async XLA Ops:
  1.4 100.1 %collective-permute-start = (f32[16,32]{1,0:T(8,128)S(1)}, f32[16,32]{1,0:T(8,128)S(1)}, u32[]{:S(2)}, u32[]{:S(2)}) collective-permute-start(f32[16,32]{1,0:T(8,128)S(1)} %get-tuple-element.11), channel_id=1, source_target_pairs={{0,4},{4,8},{8,12},{12,16},{16,20},{20,24},{24,28},{28,32},{32,36}... | collective-permute-start | bytes 6152 | tf_op jit(solution)/shard_map/ppermute | solution.py:17
  6.3 101.8 %collective-permute-start.1 = (f32[16,32]{1,0:T(8,128)S(1)}, f32[16,32]{1,0:T(8,128)S(1)}, u32[]{:S(2)}, u32[]{:S(2)}) collective-permute-start(f32[16,32]{1,0:T(8,128)S(1)} %get-tuple-element.12), channel_id=1, source_target_pairs={{4,0},{8,4},{12,8},{16,12},{20,16},{24,20},{28,24},{32,28},{36,32}... | collective-permute-start | bytes 6152 | tf_op jit(solution)/shard_map/ppermute | solution.py:19
  10.3 49.0 %copy-start.1 = (s32[64]{0:T(128)S(1)}, s32[64]{0:T(128)}, u32[]{:S(2)}) copy-start(s32[64]{0:T(128)} %param.6) | copy-start | bytes 772
  10.3 49.1 %copy-start = (s32[64]{0:T(128)S(1)}, s32[64]{0:T(128)}, u32[]{:S(2)}) copy-start(s32[64]{0:T(128)} %param.7) | copy-start | bytes 772
where the time goes:
time: 246 us; the launch traced here: 244 us
  between operations  86.5 us (35%)
  other arithmetic  69.5 us (28%)
  blocking collectives  54.1 us (22%)
  local copies, waits for them, and re-layouts  24.9 us (10%)
  starting transfers between devices  6.83 us (3%)
    all_to_all x1, blocking collectives, shards(): lax.all_to_all(resid, 'series', split_axis=1, concat_axis=0, tiled=True)  29 us
    add x1, other arithmetic, shards(): bend = bend + window * (curved[m] / fourth)  19.9 us
    add x1, other arithmetic, shards(): tilt = tilt + window * (offsets[m] / second)  19.9 us
    add x1, other arithmetic, shards(): level = level + window * (1.0 / taps)  19.9 us
    all_to_all x1, blocking collectives, from_everyone(): return lax.all_to_all(copies, axis, split_axis=0, concat_axis=0, tiled=True)  18.5 us
    unnamed x11, local copies, waits for them, and re-layouts  10.2 us
    gather x6, local copies, waits for them, and re-layouts, held_value(): return jnp.take_along_axis(field, spot, axis=1)  9.65 us
    all_to_all x1, blocking collectives, summed_on_arrival(): tiles = lax.all_to_all(split_up(shard, dim, count), axis, 0, 0, tiled=True)  6.56 us
  transfers between devices with their start and end apart: 2, of which 0 were waited for; matrix products, arithmetic and copies ran while one was open for 6% of the time, Pallas kernels for 0%

commit v1 on v0

--- a/solution.py
+++ b/solution.py
@@ -107,7 +107,15 @@
     smooth = jnp.where(inside, lv + tl * along + bd * (along * along - centre_sq), 0.0)
     slope = jnp.where(inside, HALF * (tl + 2.0 * along * bd), 0.0)
     resid = jnp.where(inside, signal - smooth, 0.0)
-    mixed = lax.all_to_all(resid, "series", split_axis=1, concat_axis=0, tiled=True)
+    ways, here = (lax.axis_size("series"), lax.axis_index("series"))
+    width_2 = resid.shape[1] // ways
+    turned = jnp.roll(resid, -here * width_2, axis=1)
+    got = [lax.slice_in_dim(turned, 0, width_2, axis=1)]
+    for far in range(1, ways):
+        sent = lax.slice_in_dim(turned, far * width_2, (far + 1) * width_2, axis=1)
+        got.append(lax.ppermute(sent, "series", [(d, (d + far) % ways) for d in range(ways)]))
+    line = jnp.concatenate(got[::-1], axis=0)
+    mixed = jnp.roll(line, (here + 1) * got[0].shape[0], axis=0)
     gram = summed_on_arrival(cross_rows(mixed, mixed), "series", 0)
     gram = over_copies(gram, "tm")
     correlation = (

time: 246 us -> 247 us (level)
  blocking collectives: 54.1 us -> 23.9 us
  waiting for transfers between devices: 0.01 us -> 25.4 us
  starting transfers between devices: 6.83 us -> 10.5 us
    all_to_all x1 -> x0, blocking collectives: 29 us -> none  [shards(): lax.all_to_all(resid, 'series', split_axis=1, concat_axis=0, tiled=True)]
    ppermute x0 -> x3, waiting for transfers between devices: none -> 25.4 us  [shards(): lax.ppermute(sent, 'series', [(d, (d + far) % ways) for d in range(ways)])]
    ppermute x0 -> x3, starting transfers between devices: none -> 3.71 us  [shards(): lax.ppermute(sent, 'series', [(d, (d + far) % ways) for d in range(ways)])]
    unnamed x11 -> x18, local copies, waits for them, and re-layouts: 10.2 us -> 10.5 us
  transfers between devices with their start and end apart: 2 -> 5, of which waited for: 0 -> 2; matrix products, arithmetic and copies ran while one was open for 6% -> 6% of each run, Pallas kernels for 0% -> 0%
where the time goes in v1:
time: 247 us; the launch traced here: 245 us
  between operations  87 us (35%)
  other arithmetic  70 us (28%)
  local copies, waits for them, and re-layouts  26.2 us (11%)
  waiting for transfers between devices  25.4 us (10%)
  blocking collectives  23.9 us (10%)
  starting transfers between devices  10.5 us (4%)
    ppermute x3, waiting for transfers between devices, shards(): lax.ppermute(sent, 'series', [(d, (d + far) % ways) for d in range(ways)])  25.4 us
    add x1, other arithmetic, shards(): tilt = tilt + window * (offsets[m] / second)  19.9 us
    add x1, other arithmetic, shards(): bend = bend + window * (curved[m] / fourth)  19.9 us
    add x1, other arithmetic, shards(): level = level + window * (1.0 / taps)  19.9 us
    all_to_all x1, blocking collectives, from_everyone(): return lax.all_to_all(copies, axis, split_axis=0, concat_axis=0, tiled=True)  17.3 us
    unnamed x18, local copies, waits for them, and re-layouts  10.5 us
    gather x6, local copies, waits for them, and re-layouts, held_value(): return jnp.take_along_axis(field, spot, axis=1)  9.65 us
    all_to_all x1, blocking collectives, summed_on_arrival(): tiles = lax.all_to_all(split_up(shard, dim, count), axis, 0, 0, tiled=True)  6.56 us
  transfers between devices with their start and end apart: 5, of which 2 were waited for; matrix products, arithmetic and copies ran while one was open for 6% of the time, Pallas kernels for 0%

profile of v1, /device:TPU:1, one launch (start us, length us, event | category | flops | bytes accessed | tf_op | source)
XLA Modules:
  0.0 244.8 jit_solution(14469922633675364502)
XLA Ops:
  0.6 0.8 fusion.19
  1.4 3.3 %collective-permute-start.1 = (f32[16,32]{1,0:T(8,128)S(1)}, f32[16,32]{1,0:T(8,128)S(1)}, u32[]{:S(2)}, u32[]{:S(2)}) collective-permute-start(f32[16,32]{1,0:T(8,128)S(1)} %get-tuple-element.15), channel_id=1, source_target_pairs={{4,0},{8,4},{12,8},{16,12},{20,16},{24,20},{28,24},{32,28},{36,32}... | collective-permute-start | bytes 6152 | tf_op jit(solution)/shard_map/ppermute | solution.py:19
  4.7 3.6 %collective-permute-start = (f32[16,32]{1,0:T(8,128)S(1)}, f32[16,32]{1,0:T(8,128)S(1)}, u32[]{:S(2)}, u32[]{:S(2)}) collective-permute-start(f32[16,32]{1,0:T(8,128)S(1)} %get-tuple-element.14), channel_id=1, source_target_pairs={{0,4},{4,8},{8,12},{12,16},{16,20},{20,24},{24,28},{28,32},{32,36}... | collective-permute-start | bytes 6152 | tf_op jit(solution)/shard_map/ppermute | solution.py:17
  8.9 3.1 %constant_dynamic-update-slice_fusion.1 = f32[16,32800]{1,0:T(8,128)} fusion(f32[16,32768]{1,0:T(8,128)} %param.5), kind=kLoop, calls=%fused_computation.32 | loop fusion | bytes 4194304
  102.2 6.4 %dynamic-update-slice.11 = f32[16,32832]{1,0:T(8,128)S(1)} dynamic-update-slice(f32[16,32832]{1,0:T(8,128)S(1)} %dynamic-update-slice.10, f32[16,32768]{1,0:T(8,128)} %param.5, s32[]{} %constant.203, s32[]{} %constant.205) | dynamic-update-slice | bytes 4194308
  109.3 19.9 %multiply_add_fusion.1 = f32[16,32800]{1,0:T(8,128)} fusion(f32[16,32800]{1,0:T(8,128)} %constant_dynamic-update-slice_fusion, f32[16,32832]{1,0:T(8,128)S(1)} %dynamic-update-slice.12, f32[16,32768]{1,0:T(8,128)} %param.5, f32[16,32]{1,0:T(8,128)S(1)} %collective-permute-done, f32[]{:T(128)S(6)} %div.236, f32[]{:T(128)S(6)} %div.235, f32[]{:T(128)S(6)} %div.234, ...), kind=kLoop, calls=%fused_computation.17 | loop fusion | flops 34636800 | bytes 71372928 | tf_op jit(solution)/shard_map/add | solution.py:76
  129.2 1.6 gather_fusion.3
  130.8 19.9 %multiply_add_fusion = f32[16,32800]{1,0:T(8,128)} fusion(f32[16,32800]{1,0:T(8,128)} %constant_dynamic-update-slice_fusion, f32[16,32832]{1,0:T(8,128)S(1)} %dynamic-update-slice.12, f32[16,32768]{1,0:T(8,128)} %param.5, f32[16,32]{1,0:T(8,128)S(1)} %collective-permute-done, f32[]{:T(128)S(6)} %div.270, f32[]{:T(128)S(6)} %div.269, f32[]{:T(128)S(6)} %div.268, ...), kind=kLoop, calls=%fused_computation.16 | loop fusion | flops 34636800 | bytes 71372928 | tf_op jit(solution)/shard_map/add | solution.py:77
  150.7 1.6 gather_fusion.5
  152.3 1.6 gather_fusion.4
  153.9 1.6 gather_fusion.2
  155.5 19.9 %add_multiply_fusion = f32[16,32800]{1,0:T(8,128)} fusion(f32[16,32800]{1,0:T(8,128)} %constant_dynamic-update-slice_fusion, f32[16,32832]{1,0:T(8,128)S(1)} %dynamic-update-slice.12, f32[16,32768]{1,0:T(8,128)} %param.5, f32[16,32]{1,0:T(8,128)S(1)} %collective-permute-done), kind=kLoop, calls=%fused_computation.15 | loop fusion | flops 17843200 | bytes 71372800 | tf_op jit(solution)/shard_map/add | solution.py:75
  175.4 1.6 gather_fusion.1
  177.0 1.6 gather_fusion
  178.6 6.0 %subtract_select_fusion = (f32[16,32768]{1,0:T(8,128)S(1)}, f32[16,32768]{1,0:T(8,128)}, f32[16,32768]{1,0:T(8,128)}) fusion(f32[16,32768]{1,0:T(8,128)} %param.5, s32[32768]{0:T(1024)S(1)} %iota_add_fusion, s32[16]{0:T(128)S(1)} %get-tuple-element.9, s32[16]{0:T(128)S(1)} %get-tuple-element.7, f32[]{:T(128)S(6)} %div.237, f32[16,32800]{1,0:T(8,128)} %multiply_add_fusion, ...), kind=kLoop, calls=%fused_computation.24 | loop fusion | flops 15204352 | bytes 14811780 | tf_op jit(solution)/shard_map/jit(_where)/select_n | solution.py:109
  185.2 1.1 fusion.18
  186.3 2.6 %collective-permute-start.2 = (f32[16,8192]{1,0:T(8,128)}, f32[16,8192]{1,0:T(8,128)S(1)}, u32[]{:S(2)}, u32[]{:S(2)}) collective-permute-start(f32[16,8192]{1,0:T(8,128)} %get-tuple-element.13), channel_id=1, source_target_pairs={{0,3},{1,0},{2,1},{3,2},{4,7},{5,4},{6,5},{7,6},{8,11},{9,8},{10,9... | collective-permute-start | bytes 1572872 | tf_op jit(solution)/shard_map/ppermute | solution.py:116
  189.2 0.8 collective-permute-start.4
  190.0 21.6 %collective-permute-done.2 = f32[16,8192]{1,0:T(8,128)S(1)} collective-permute-done((f32[16,8192]{1,0:T(8,128)}, f32[16,8192]{1,0:T(8,128)S(1)}, u32[]{:S(2)}, u32[]{:S(2)}) %collective-permute-start.2) | collective-permute-done | bytes 524320 | tf_op jit(solution)/shard_map/ppermute | solution.py:116
  211.7 3.8 %collective-permute-done.4 = f32[16,8192]{1,0:T(8,128)S(1)} collective-permute-done((f32[16,8192]{1,0:T(8,128)S(1)}, f32[16,8192]{1,0:T(8,128)S(1)}, u32[]{:S(2)}, u32[]{:S(2)}) %collective-permute-start.4) | collective-permute-done | bytes 524320 | tf_op jit(solution)/shard_map/ppermute | solution.py:116
  215.7 1.8 fusion.4
  217.6 6.6 %all_to_all.10 = f32[4,1,1024]{2,1,0:T(1,128)S(1)} all-to-all(f32[4,1,1024]{2,1,0:T(1,128)S(1)} %reshape.135), channel_id=1, replica_groups=mesh['tm'=32,'series'=4] {'series'}, dimensions={0} | all-to-all | bytes 32768 | tf_op jit(solution)/shard_map/all_to_all | solution.py:33
  225.7 17.3 %all_to_all.11 = f32[32,1,1024]{2,1,0:T(1,128)S(1)} all-to-all(f32[32,1,1024]{2,1,0:T(1,128)S(1)} %reshape.137), channel_id=1, replica_groups=mesh['tm'=32,'series'=4] {'tm'}, dimensions={0} | all-to-all | bytes 262144 | tf_op jit(solution)/shard_map/all_to_all | solution.py:39
  243.0 1.0 reduce.1
  (49 shorter events, 9.1 us)
Async XLA Ops:
  1.4 107.1 %collective-permute-start.1 = (f32[16,32]{1,0:T(8,128)S(1)}, f32[16,32]{1,0:T(8,128)S(1)}, u32[]{:S(2)}, u32[]{:S(2)}) collective-permute-start(f32[16,32]{1,0:T(8,128)S(1)} %get-tuple-element.15), channel_id=1, source_target_pairs={{4,0},{8,4},{12,8},{16,12},{20,16},{24,20},{28,24},{32,28},{36,32}... | collective-permute-start | bytes 6152 | tf_op jit(solution)/shard_map/ppermute | solution.py:19
  4.7 97.2 %collective-permute-start = (f32[16,32]{1,0:T(8,128)S(1)}, f32[16,32]{1,0:T(8,128)S(1)}, u32[]{:S(2)}, u32[]{:S(2)}) collective-permute-start(f32[16,32]{1,0:T(8,128)S(1)} %get-tuple-element.14), channel_id=1, source_target_pairs={{0,4},{4,8},{8,12},{12,16},{16,20},{20,24},{24,28},{28,32},{32,36}... | collective-permute-start | bytes 6152 | tf_op jit(solution)/shard_map/ppermute | solution.py:17
  8.9 7.3 %copy-start = (s32[64]{0:T(128)S(1)}, s32[64]{0:T(128)}, u32[]{:S(2)}) copy-start(s32[64]{0:T(128)} %param.7) | copy-start | bytes 772
  8.9 7.4 %copy-start.1 = (s32[64]{0:T(128)S(1)}, s32[64]{0:T(128)}, u32[]{:S(2)}) copy-start(s32[64]{0:T(128)} %param.6) | copy-start | bytes 772
  186.3 25.3 %collective-permute-start.2 = (f32[16,8192]{1,0:T(8,128)}, f32[16,8192]{1,0:T(8,128)S(1)}, u32[]{:S(2)}, u32[]{:S(2)}) collective-permute-start(f32[16,8192]{1,0:T(8,128)} %get-tuple-element.13), channel_id=1, source_target_pairs={{0,3},{1,0},{2,1},{3,2},{4,7},{5,4},{6,5},{7,6},{8,11},{9,8},{10,9... | collective-permute-start | bytes 1572872 | tf_op jit(solution)/shard_map/ppermute | solution.py:116
  188.9 22.8 %collective-permute-start.3 = (f32[16,8192]{1,0:T(8,128)}, f32[16,8192]{1,0:T(8,128)S(1)}, u32[]{:S(2)}, u32[]{:S(2)}) collective-permute-start(f32[16,8192]{1,0:T(8,128)} %get-tuple-element.12), channel_id=1, source_target_pairs={{0,2},{1,3},{2,0},{3,1},{4,6},{5,7},{6,4},{7,5},{8,10},{9,11},{10,... | collective-permute-start | bytes 1572872 | tf_op jit(solution)/shard_map/ppermute | solution.py:116
  189.2 26.2 %collective-permute-start.4 = (f32[16,8192]{1,0:T(8,128)S(1)}, f32[16,8192]{1,0:T(8,128)S(1)}, u32[]{:S(2)}, u32[]{:S(2)}) collective-permute-start(f32[16,8192]{1,0:T(8,128)S(1)} %get-tuple-element.11), channel_id=1, source_target_pairs={{0,1},{1,2},{2,3},{3,0},{4,5},{5,6},{6,7},{7,4},{8,9},{9,10},{10,1... | collective-permute-start | bytes 1572872 | tf_op jit(solution)/shard_map/ppermute | solution.py:116
